TPU v7x, 32 devices: a whole 2x2x4 slice. The times are simulated.
32 devices in a mesh: dp: 8 (over z, y), grp: 4 (over x, core).
Axes of the slice: x: 2, y: 2, z: 4, core: 2. Of those that a mesh axis runs over, the one named last changes fastest.
Arguments:
- activations: bfloat16 [32, 512, 768], P('dp', None, 'grp'), may hold values from -6 to 6, as said below
- cotangent: bfloat16 [32, 512, 768], P('dp', None, 'grp'), may hold values from -6 to 6
- lengths: int32 [32], P('dp'), may hold values from 64 to 512
- triple_weight: bfloat16 [2, 4, 192, 576], P(None, 'grp'), may hold values from -0.25980762 to 0.25980762, as said below
- triple_bias: float32 [2, 2, 768], P(None, None, 'grp'), may hold values from -1.8 to 1.8, as said below
- output_weight: bfloat16 [2, 768, 768], replicated, may hold values from -1.75 to 1.75
- output_bias: float32 [2, 768], replicated, may hold values from -1.75 to 1.75
- first_gain: float32 [2, 768], replicated, may hold values from 0.25 to 1.75
- first_shift: float32 [2, 768], replicated, may hold values from -1.75 to 1.75
- widen_weight: bfloat16 [2, 4, 192, 768], P(None, 'grp'), may hold values from -0.4375 to 0.4375
- widen_bias: float32 [2, 3072], P(None, 'grp'), may hold values from -1.75 to 1.75
- shrink_weight: bfloat16 [2, 4, 768, 192], P(None, 'grp'), may hold values from -0.21875 to 0.21875
- narrow_bias: float32 [2, 768], P(None, 'grp'), may hold values from -1.75 to 1.75
- second_gain: float32 [2, 768], P(None, 'grp'), may hold values from 0.25 to 1.75
- second_shift: float32 [2, 768], P(None, 'grp'), may hold values from -1.75 to 1.75
Outputs:
- layer_output: bfloat16 [32, 512, 768], P('dp', None, 'grp')
- input_gradient: float32 [32, 512, 768], P('dp', None, 'grp')
- triple_weight_gradient: float32 [2, 4, 192, 576], P(None, 'grp')
- triple_bias_gradient: float32 [2, 2, 768], P(None, None, 'grp')
- output_weight_gradient: float32 [2, 768, 768], replicated
- output_bias_gradient: float32 [2, 768], replicated
- first_gain_gradient: float32 [2, 768], replicated
- first_shift_gradient: float32 [2, 768], replicated
- widen_weight_gradient: float32 [2, 4, 192, 768], P(None, 'grp')
- widen_bias_gradient: float32 [2, 3072], P(None, 'grp')
- narrow_weight_gradient: float32 [2, 4, 768, 192], P(None, 'grp')
- narrow_bias_gradient: float32 [2, 768], P(None, 'grp')
- second_norm_gain_gradient: float32 [2, 768], P(None, 'grp')
- second_shift_gradient: float32 [2, 768], P(None, 'grp')
Inputs may be any that keep to these rules, and one draw needn't show every extreme that they name: `activations`: independent entries of order one. `triple_weight`: independent entries with deviation about 192 ** -0.5. `triple_bias`: independent entries with deviation about 0.3.
All inputs are finite; a program needn't handle non-finite values.
Results may differ from a plain program's by a relative error of at most 0.015.
Values may be sent and summed in bfloat16 or wider, within the bound.
A program may use at most 192 MiB of HBM per device.

v0:
```python
import math
import jax
import jax.numpy as jnp
from jax import lax
from jax.sharding import PartitionSpec as P

HEAD = 64
EPSILON = 1e-05
MASKED = -1e30


def contract_rows(left, right):
    return lax.dot_general(
        left, right, (((0,), (0,)), ((), ())), preferred_element_type=jnp.float32
    )


def contract_cols(left, weight):
    return lax.dot_general(
        left, weight, (((1,), (1,)), ((), ())), preferred_element_type=jnp.float32
    )


def split_heads(block):
    return block.reshape(block.shape[0], block.shape[1] // HEAD, HEAD)


def score_block(queries, keys, length):
    scores = jnp.einsum(
        "qhd,khd->hqk", split_heads(queries), split_heads(keys), preferred_element_type=jnp.float32
    ) * HEAD ** (-0.5)
    visible = jnp.arange(keys.shape[0]) < length
    return jnp.where(visible[None, None, :], scores, MASKED)


def attend_forward(queries, keys, values, lengths):

    def single(inputs):
        query_one, key_one, value_one, length = inputs
        scores = score_block(query_one, key_one, length)
        highest = jnp.max(scores, axis=-1, keepdims=True)
        expon = jnp.exp(scores - highest)
        totals = jnp.sum(expon, axis=-1, keepdims=True)
        weights = (expon / totals).astype(jnp.bfloat16)
        mixed = jnp.einsum(
            "hqk,khd->qhd", weights, split_heads(value_one), preferred_element_type=jnp.float32
        )
        return (mixed.reshape(query_one.shape).astype(jnp.bfloat16), highest, totals)

    return lax.map(single, (queries, keys, values, lengths))


def attend_backward(queries, keys, values, outgrad, highest, totals, lengths):

    def single(inputs):
        query_one, key_one, value_one, grad_one, top, total, length = inputs
        scores = score_block(query_one, key_one, length)
        probs = jnp.exp(scores - top) / total
        weights = probs.astype(jnp.bfloat16)
        grad_heads = split_heads(grad_one)
        grad_probs = jnp.einsum(
            "qhd,khd->hqk", grad_heads, split_heads(value_one), preferred_element_type=jnp.float32
        )
        inner = jnp.sum(probs * grad_probs, axis=-1, keepdims=True)
        grad_scores = (probs * (grad_probs - inner)).astype(jnp.bfloat16)
        factor = HEAD ** (-0.5)
        query_grad = (
            jnp.einsum(
                "hqk,khd->qhd",
                grad_scores,
                split_heads(key_one),
                preferred_element_type=jnp.float32,
            )
            * factor
        )
        key_grad = (
            jnp.einsum(
                "hqk,qhd->khd",
                grad_scores,
                split_heads(query_one),
                preferred_element_type=jnp.float32,
            )
            * factor
        )
        value_grad = jnp.einsum(
            "hqk,qhd->khd", weights, grad_heads, preferred_element_type=jnp.float32
        )
        shape = query_one.shape
        return (
            query_grad.reshape(shape).astype(jnp.bfloat16),
            key_grad.reshape(shape).astype(jnp.bfloat16),
            value_grad.reshape(shape).astype(jnp.bfloat16),
        )

    return lax.map(single, (queries, keys, values, outgrad, highest, totals, lengths))


def gelu_slope(values):
    return 0.5 * (1.0 + lax.erf(values / math.sqrt(2.0))) + values * jnp.exp(
        -0.5 * values * values
    ) / math.sqrt(2.0 * math.pi)


def layer_forward(inputs, lengths, params, layer_params):
    (
        triple_weight,
        triple_bias,
        output_weight,
        output_bias,
        first_gain,
        first_shift,
        widen_weight,
        widen_bias,
        shrink_weight,
        narrow_bias,
        second_gain,
        second_shift,
    ) = params
    group_width = inputs.shape[-1]
    rows = inputs.reshape(-1, group_width)
    projected = jnp.dot(rows, triple_weight[layer_params, 0], preferred_element_type=jnp.float32)
    queries = (
        (projected[:, :group_width] + triple_bias[layer_params, 0])
        .astype(jnp.bfloat16)
        .reshape(inputs.shape)
    )
    keys = projected[:, group_width : 2 * group_width].astype(jnp.bfloat16).reshape(inputs.shape)
    values = (
        (projected[:, 2 * group_width :] + triple_bias[layer_params, 1])
        .astype(jnp.bfloat16)
        .reshape(inputs.shape)
    )
    queries, keys, values, residual = (
        lax.all_to_all(queries, "grp", split_axis=0, concat_axis=2, tiled=True),
        lax.all_to_all(keys, "grp", split_axis=0, concat_axis=2, tiled=True),
        lax.all_to_all(values, "grp", split_axis=0, concat_axis=2, tiled=True),
        lax.all_to_all(inputs, "grp", split_axis=0, concat_axis=2, tiled=True),
    )
    local = queries.shape[0]
    mine = lax.dynamic_slice_in_dim(lengths, lax.axis_index("grp") * local, local)
    attended, highest, totals = attend_forward(queries, keys, values, mine)
    width = attended.shape[-1]
    flat = attended.reshape(-1, width)
    before = (
        residual.reshape(-1, width).astype(jnp.float32)
        + jnp.dot(flat, output_weight[layer_params], preferred_element_type=jnp.float32)
        + output_bias[layer_params]
    )
    center = before - jnp.mean(before, axis=-1, keepdims=True)
    first_inverse = lax.rsqrt(jnp.mean(center * center, axis=-1, keepdims=True) + EPSILON)
    first_normed = center * first_inverse
    hidden = (
        (first_normed * first_gain[layer_params] + first_shift[layer_params])
        .astype(jnp.bfloat16)
        .reshape(attended.shape)
    )
    hidden_group = lax.all_to_all(hidden, "grp", split_axis=2, concat_axis=0, tiled=True)
    group_rows = hidden_group.reshape(-1, group_width)
    widened = (
        jnp.dot(group_rows, widen_weight[layer_params, 0], preferred_element_type=jnp.float32)
        + widen_bias[layer_params]
    )
    gelu_output = jax.nn.gelu(widened, approximate=False).astype(jnp.bfloat16)
    after = (
        group_rows.astype(jnp.float32)
        + jnp.dot(gelu_output, shrink_weight[layer_params, 0], preferred_element_type=jnp.float32)
        + narrow_bias[layer_params]
    )
    row_sum = jnp.sum(after, axis=-1)
    row_square = jnp.sum(after * after, axis=-1)
    total_sum, total_square = lax.psum((row_sum, row_square), "grp")
    average = (total_sum / width)[:, None]
    variance = (total_square / width)[:, None] - average * average
    second_inverse = lax.rsqrt(variance + EPSILON)
    second_normed = (after - average) * second_inverse
    output = (second_normed * second_gain[layer_params] + second_shift[layer_params]).reshape(
        inputs.shape
    )
    kept = (
        inputs,
        queries,
        keys,
        values,
        mine,
        highest,
        totals,
        attended,
        first_normed,
        first_inverse,
        group_rows,
        widened,
        gelu_output,
        second_normed,
        second_inverse,
    )
    return (output, kept)


def layer_backward(outgrad, params, layer_params, kept):
    (
        triple_weight,
        triple_bias,
        output_weight,
        output_bias,
        first_gain,
        first_shift,
        widen_weight,
        widen_bias,
        shrink_weight,
        narrow_bias,
        second_gain,
        second_shift,
    ) = params
    (
        inputs,
        queries,
        keys,
        values,
        mine,
        highest,
        totals,
        attended,
        first_normed,
        first_inverse,
        group_rows,
        widened,
        gelu_output,
        second_normed,
        second_inverse,
    ) = kept
    group_width = inputs.shape[-1]
    width = attended.shape[-1]
    grad_rows = outgrad.reshape(-1, group_width)
    scaled = grad_rows * second_gain[layer_params]
    part_sum = jnp.sum(scaled, axis=-1)
    part_cross = jnp.sum(scaled * second_normed, axis=-1)
    total_sum, total_cross = lax.psum((part_sum, part_cross), "grp")
    grad_after = second_inverse * (
        scaled - (total_sum / width)[:, None] - second_normed * (total_cross / width)[:, None]
    )
    second_gain_grad = jnp.sum(grad_rows * second_normed, axis=0)
    second_shift_grad = jnp.sum(grad_rows, axis=0)
    narrow_rounded = grad_after.astype(jnp.bfloat16)
    narrow_weight_grad = contract_rows(gelu_output, narrow_rounded)
    narrow_bias_grad = jnp.sum(narrow_rounded.astype(jnp.float32), axis=0)
    gelu_output_gradient = contract_cols(narrow_rounded, shrink_weight[layer_params, 0])
    widened_grad = (gelu_output_gradient * gelu_slope(widened)).astype(jnp.bfloat16)
    widen_weight_grad = contract_rows(group_rows, widened_grad)
    widen_bias_grad = jnp.sum(widened_grad.astype(jnp.float32), axis=0)
    hidden_grad = (grad_after + contract_cols(widened_grad, widen_weight[layer_params, 0])).astype(
        jnp.bfloat16
    )
    hidden_seq = lax.all_to_all(
        hidden_grad.reshape(inputs.shape), "grp", split_axis=0, concat_axis=2, tiled=True
    )
    seq_rows = hidden_seq.reshape(-1, width).astype(jnp.float32)
    first_gain_grad = jnp.sum(seq_rows * first_normed, axis=0)
    first_shift_grad = jnp.sum(seq_rows, axis=0)
    scaled_first = seq_rows * first_gain[layer_params]
    grad_before = first_inverse * (
        scaled_first
        - jnp.mean(scaled_first, axis=-1, keepdims=True)
        - first_normed * jnp.mean(scaled_first * first_normed, axis=-1, keepdims=True)
    )
    before_rounded = grad_before.astype(jnp.bfloat16)
    flat = attended.reshape(-1, width)
    output_weight_grad = contract_rows(flat, before_rounded)
    output_bias_grad = jnp.sum(before_rounded.astype(jnp.float32), axis=0)
    attended_grad = (
        contract_cols(before_rounded, output_weight[layer_params])
        .astype(jnp.bfloat16)
        .reshape(attended.shape)
    )
    residual_grad = before_rounded.reshape(attended.shape)
    query_seq, key_seq, value_seq = attend_backward(
        queries, keys, values, attended_grad, highest, totals, mine
    )
    query_grad, key_grad, value_grad, input_part = (
        lax.all_to_all(query_seq, "grp", split_axis=2, concat_axis=0, tiled=True),
        lax.all_to_all(key_seq, "grp", split_axis=2, concat_axis=0, tiled=True),
        lax.all_to_all(value_seq, "grp", split_axis=2, concat_axis=0, tiled=True),
        lax.all_to_all(residual_grad, "grp", split_axis=2, concat_axis=0, tiled=True),
    )
    triple_grad = jnp.concatenate(
        [
            query_grad.reshape(-1, group_width),
            key_grad.reshape(-1, group_width),
            value_grad.reshape(-1, group_width),
        ],
        axis=-1,
    )
    triple_weight_grad = contract_rows(inputs.reshape(-1, group_width), triple_grad)
    triple_bias_grad = jnp.stack(
        [
            jnp.sum(query_grad.reshape(-1, group_width).astype(jnp.float32), axis=0),
            jnp.sum(value_grad.reshape(-1, group_width).astype(jnp.float32), axis=0),
        ]
    )
    input_grad = contract_cols(triple_grad, triple_weight[layer_params, 0]) + input_part.reshape(
        -1, group_width
    ).astype(jnp.float32)
    grads = (
        triple_weight_grad[None],
        triple_bias_grad,
        output_weight_grad,
        output_bias_grad,
        first_gain_grad,
        first_shift_grad,
        widen_weight_grad[None],
        widen_bias_grad,
        narrow_weight_grad[None],
        narrow_bias_grad,
        second_gain_grad,
        second_shift_grad,
    )
    return (input_grad.reshape(inputs.shape), grads)


def shards(
    activations,
    cotangent,
    lengths,
    triple_weight,
    triple_bias,
    output_weight,
    output_bias,
    first_gain,
    first_shift,
    widen_weight,
    widen_bias,
    shrink_weight,
    narrow_bias,
    second_gain,
    second_shift,
):
    params = (
        triple_weight,
        triple_bias,
        output_weight,
        output_bias,
        first_gain,
        first_shift,
        widen_weight,
        widen_bias,
        shrink_weight,
        narrow_bias,
        second_gain,
        second_shift,
    )
    depth = triple_weight.shape[0]
    current = activations
    stored = []
    kept_list = []
    final = None
    for layer_params in range(depth):
        stored.append(current)
        result, kept = layer_forward(current, lengths, params, layer_params)
        kept_list.append(kept)
        final = result
        current = result.astype(jnp.bfloat16)
    outgrad = cotangent.astype(jnp.float32)
    collected = [None] * depth
    for layer_params in reversed(range(depth)):
        replayed, kept = layer_forward(stored[layer_params], lengths, params, layer_params)
        outgrad, layer_param_gradients = layer_backward(outgrad, params, layer_params, kept)
        collected[layer_params] = layer_param_gradients
    stacked = [
        jnp.stack([collected[layer_params][member] for layer_params in range(depth)])
        for member in range(12)
    ]
    group_totals = lax.psum(
        (
            stacked[0],
            stacked[1],
            stacked[6],
            stacked[7],
            stacked[8],
            stacked[9],
            stacked[10],
            stacked[11],
        ),
        "dp",
    )
    shared_totals = lax.psum((stacked[2], stacked[3], stacked[4], stacked[5]), ("dp", "grp"))
    return (
        final.astype(jnp.bfloat16),
        outgrad,
        group_totals[0],
        group_totals[1],
        shared_totals[0],
        shared_totals[1],
        shared_totals[2],
        shared_totals[3],
        group_totals[2],
        group_totals[3],
        group_totals[4],
        group_totals[5],
        group_totals[6],
        group_totals[7],
    )


def solution(mesh):
    in_specs = (
        P("dp", None, "grp"),
        P("dp", None, "grp"),
        P("dp"),
        P(None, "grp", None, None),
        P(None, None, "grp"),
        P(),
        P(),
        P(),
        P(),
        P(None, "grp", None, None),
        P(None, "grp"),
        P(None, "grp", None, None),
        P(None, "grp"),
        P(None, "grp"),
        P(None, "grp"),
    )
    out_specs = (
        P("dp", None, "grp"),
        P("dp", None, "grp"),
        P(None, "grp", None, None),
        P(None, None, "grp"),
        P(),
        P(),
        P(),
        P(),
        P(None, "grp", None, None),
        P(None, "grp"),
        P(None, "grp", None, None),
        P(None, "grp"),
        P(None, "grp"),
        P(None, "grp"),
    )
    return jax.shard_map(shards, mesh=mesh, in_specs=in_specs, out_specs=out_specs, check_vma=False)
```

profile of v0, /device:TPU:0, one launch (start us, length us, event | category | flops | bytes accessed | tf_op | source)
XLA Modules:
  0.0 857.9 jit_solution(8457950099970390052)
XLA Ops:
  31.4 6.9 all-to-all-done.3
  45.1 9.1 %all-to-all-done.2 = bf16[4,512,192]{1,2,0:T(8,128)(2,1)} async-done(((bf16[4,512,192]{1,2,0:T(8,128)(2,1)}), bf16[4,512,192]{1,2,0:T(8,128)(2,1)}, u32[]{:S(2)}, u32[]{:S(2)}) %all-to-all-start.2) | async-done | bytes 786464 | tf_op jit(solution)/shard_map/all_to_all | solution.py:134
  57.7 10.6 %fusion.129 = (f32[12,512]{1,0:T(8,128)S(1)}, f32[12,512,512]{1,2,0:T(8,128)}) fusion(pred[512]{0:T(512)(128)(4,1)S(1)} %iota_compare_fusion, bf16[512,12,64]{0,2,1:T(8,128)(2,1)} %bitcast.12, bf16[512,12,64]{0,2,1:T(8,128)(2,1)S(1)} %bitcast.431), kind=kOutput, calls=%fused_computation.281 | convolution fusion | flops 415236608 | bytes 14180864 | tf_op jit(solution)/shard_map/while/body/eval_jaxpr/sub | solution.py:42
  91.6 10.4 %all-to-all-done.4 = bf16[4,2,49152]{2,1,0:T(2,128)(2,1)S(1)} async-done(((bf16[4,2,49152]{2,1,0:T(2,128)(2,1)}), bf16[4,2,49152]{2,1,0:T(2,128)(2,1)S(1)}, u32[]{:S(2)}, u32[]{:S(2)}) %all-to-all-start.4) | async-done | bytes 786464 | tf_op jit(solution)/shard_map/all_to_all | solution.py:157
  103.8 15.9 %fusion.6 = (bf16[2048,768]{1,0:T(8,128)(2,1)S(1)}, f32[2048,768]{1,0:T(8,128)}) fusion(f32[768]{0:T(1024)S(1)} %get-tuple-element.241, bf16[2048,192]{0,1:T(8,128)(2,1)S(1)} %bitcast.493, bf16[2,1,192,768]{3,2,1,0:T(8,128)(2,1)S(1)} %copy-done.66), kind=kOutput, calls=%fused_computation.18 | convolution fusion | flops 707788800 | bytes 10522624 | tf_op jit(solution)/shard_map/dot_general | solution.py:160
  121.4 10.1 %all-reduce.6 = (f32[2048]{0:T(1024)S(1)}, f32[2048]{0:T(1024)S(1)}) all-reduce(f32[2048]{0:T(1024)S(1)} %get-tuple-element.233, f32[2048]{0:T(1024)S(1)} %get-tuple-element.232), channel_id=1, replica_groups=mesh['dp'=8,'grp'=4] {'grp'}, use_global_device_ids=true, to_apply=%region_7.8 | all-reduce | flops 4096 | bytes 32768 | tf_op jit(solution)/shard_map/psum | solution.py:171
  155.4 8.5 all-to-all-done.8
  171.0 8.9 %all-to-all-done.7 = bf16[4,512,192]{1,2,0:T(8,128)(2,1)} async-done(((bf16[4,512,192]{1,2,0:T(8,128)(2,1)}), bf16[4,512,192]{1,2,0:T(8,128)(2,1)}, u32[]{:S(2)}, u32[]{:S(2)}) %all-to-all-start.7) | async-done | bytes 786464 | tf_op jit(solution)/shard_map/all_to_all | solution.py:134
  183.4 10.5 %fusion.131 = (f32[12,512]{1,0:T(8,128)S(1)}, f32[12,512,512]{1,2,0:T(8,128)}) fusion(pred[512]{0:T(512)(128)(4,1)S(1)} %iota_compare_fusion, bf16[512,12,64]{0,2,1:T(8,128)(2,1)} %bitcast.37, bf16[512,12,64]{0,2,1:T(8,128)(2,1)S(1)} %bitcast.433), kind=kOutput, calls=%fused_computation.283 | convolution fusion | flops 415236608 | bytes 14180864 | tf_op jit(solution)/shard_map/while/body/eval_jaxpr/sub | solution.py:42
  221.9 10.4 %all-to-all-done.9 = bf16[4,2,49152]{2,1,0:T(2,128)(2,1)} async-done(((bf16[4,2,49152]{2,1,0:T(2,128)(2,1)}), bf16[4,2,49152]{2,1,0:T(2,128)(2,1)}, u32[]{:S(2)}, u32[]{:S(2)}) %all-to-all-start.9) | async-done | bytes 786464 | tf_op jit(solution)/shard_map/all_to_all | solution.py:157
  238.5 15.8 %fusion.9 = (bf16[2048,768]{1,0:T(8,128)(2,1)S(1)}, f32[2048,768]{1,0:T(8,128)}) fusion(f32[768]{0:T(1024)S(1)} %get-tuple-element.240, bf16[2048,192]{0,1:T(8,128)(2,1)S(1)} %bitcast.497, bf16[2,1,192,768]{3,2,1,0:T(8,128)(2,1)S(1)} %copy-done.67), kind=kOutput, calls=%fused_computation.21 | convolution fusion | flops 707788800 | bytes 10522624 | tf_op jit(solution)/shard_map/dot_general | solution.py:160
  256.7 10.3 %all-reduce.5 = (f32[2048]{0:T(1024)S(1)}, f32[2048]{0:T(1024)S(1)}) all-reduce(f32[2048]{0:T(1024)S(1)} %get-tuple-element.231, f32[2048]{0:T(1024)S(1)} %get-tuple-element.230), channel_id=1, replica_groups=mesh['dp'=8,'grp'=4] {'grp'}, use_global_device_ids=true, to_apply=%region_15.16 | all-reduce | flops 4096 | bytes 32768 | tf_op jit(solution)/shard_map/psum | solution.py:171
  269.4 10.3 %all-reduce.4 = (f32[2048]{0:T(1024)S(1)}, f32[2048]{0:T(1024)S(1)}) all-reduce(f32[2048]{0:T(1024)S(1)} %get-tuple-element.223, f32[2048]{0:T(1024)S(1)} %bitcast.523), channel_id=1, replica_groups=mesh['dp'=8,'grp'=4] {'grp'}, use_global_device_ids=true, to_apply=%region_19.20 | all-reduce | flops 4096 | bytes 32768 | tf_op jit(solution)/shard_map/psum | solution.py:237
  297.1 11.6 %all-to-all-done.10 = bf16[4,512,192]{1,2,0:T(8,128)(2,1)} async-done(((bf16[4,512,192]{1,2,0:T(8,128)(2,1)}), bf16[4,512,192]{1,2,0:T(8,128)(2,1)}, u32[]{:S(2)}, u32[]{:S(2)}) %all-to-all-start.10) | async-done | bytes 786464 | tf_op jit(solution)/shard_map/all_to_all | solution.py:253
  322.3 6.9 fusion.70
  342.8 11.6 %multiply_reduce_fusion.1 = (f32[12,512]{1,0:T(8,128)S(1)}, f32[12,512,512]{1,2,0:T(8,128)}) fusion(f32[12,512,512]{1,2,0:T(8,128)} %get-tuple-element.302, f32[12,512]{1,0:T(8,128)S(1)} %get-tuple-element.301, bf16[512,12,64]{0,2,1:T(8,128)(2,1)} %bitcast.513, bf16[512,12,64]{0,2,1:T(8,128)(2,1)} %bitcast.510), kind=kOutput, calls=%fused_computation.5 | convolution fusion | flops 412084224 | bytes 26787840 | tf_op jit(solution)/shard_map/while/body/eval_jaxpr/qhd,khd->hqk/dot_general | solution.py:61
  369.7 9.6 %multiply_convert_fusion.1 = bf16[12,512,512]{1,2,0:T(8,128)(2,1)S(1)} fusion(f32[12,512,512]{1,2,0:T(8,128)} %get-tuple-element.309, f32[12,512]{1,0:T(8,128)S(1)} %get-tuple-element.308, f32[12,512,512]{1,2,0:T(8,128)} %get-tuple-element.302, f32[12,512]{1,0:T(8,128)S(1)} %get-tuple-element.301), kind=kLoop, calls=%fused_computation.4 | loop fusion | flops 12582912 | bytes 31506432 | tf_op jit(solution)/shard_map/while/body/eval_jaxpr/convert_element_type | solution.py:65
  440.9 11.9 %all-reduce.3 = (f32[2048]{0:T(1024)S(1)}, f32[2048]{0:T(1024)S(1)}) all-reduce(f32[2048]{0:T(1024)S(1)} %get-tuple-element.221, f32[2048]{0:T(1024)S(1)} %get-tuple-element.228), channel_id=1, replica_groups=mesh['dp'=8,'grp'=4] {'grp'}, use_global_device_ids=true, to_apply=%region_26.27 | all-reduce | flops 4096 | bytes 32768 | tf_op jit(solution)/shard_map/psum | solution.py:237
  495.9 8.9 %multiply_reduce_fusion = (f32[12,512]{1,0:T(8,128)S(1)}, f32[12,512,512]{1,2,0:T(8,128)}) fusion(f32[12,512,512]{1,2,0:T(8,128)} %get-tuple-element.295, f32[12,512]{1,0:T(8,128)S(1)} %copy-done.81, bf16[512,12,64]{0,2,1:T(8,128)(2,1)S(1)} %bitcast.515, bf16[512,12,64]{0,2,1:T(8,128)(2,1)S(1)} %bitcast.508), kind=kOutput, calls=%fused_computation.3 | convolution fusion | flops 412084224 | bytes 26787840 | tf_op jit(solution)/shard_map/while/body/eval_jaxpr/qhd,khd->hqk/dot_general | solution.py:61
  517.2 9.6 %multiply_convert_fusion = bf16[12,512,512]{1,2,0:T(8,128)(2,1)S(1)} fusion(f32[12,512,512]{1,2,0:T(8,128)} %get-tuple-element.312, f32[12,512]{1,0:T(8,128)S(1)} %get-tuple-element.311, f32[12,512,512]{1,2,0:T(8,128)} %get-tuple-element.295, f32[12,512]{1,0:T(8,128)S(1)} %copy-done.81), kind=kLoop, calls=%fused_computation.2 | loop fusion | flops 12582912 | bytes 31506432 | tf_op jit(solution)/shard_map/while/body/eval_jaxpr/convert_element_type | solution.py:65
  558.1 7.5 reduce.35
  614.4 47.1 %all-reduce = (f32[2,768]{1,0:T(2,128)}, f32[2,768]{1,0:T(2,128)}, f32[2,768]{1,0:T(2,128)}) all-reduce(f32[2,768]{1,0:T(2,128)S(1)} %pad_maximum_fusion.4, f32[2,768]{1,0:T(2,128)S(1)} %pad_maximum_fusion.5, f32[2,768]{1,0:T(2,128)S(1)} %pad_maximum_fusion.6), channel_id=1, replica_groups=mesh['dp'=8,'grp'=4] {'dp','grp'}, use_global_device_ids=true, to_apply=%region_39.40 | all-reduce | flops 4608 | bytes 36864 | tf_op jit(solution)/shard_map/psum | solution.py:384
  668.6 37.8 %all-reduce.1 = (f32[2,2,192]{2,1,0:T(2,128)}, f32[2,768]{1,0:T(2,128)}, f32[2,192]{1,0:T(2,128)}, f32[2,192]{1,0:T(2,128)}, f32[2,192]{1,0:T(2,128)}) all-reduce(f32[2,2,192]{2,1,0:T(2,128)S(1)} %pad_maximum_fusion.8, f32[2,768]{1,0:T(2,128)S(1)} %pad_maximum_fusion.7, ...), channel_id=1, replica_groups=mesh['dp'=8,'grp'=4] {'dp'}, use_global_device_ids=true, to_apply=%region_35.36 | all-reduce | flops 3456 | bytes 27648 | tf_op jit(solution)/shard_map/psum | solution.py:371
  706.3 134.4 %all-reduce.12.cloned.1.call-done = (f32[2,1,192,576]{3,2,1,0:T(8,128)}, f32[2,1,192,768]{3,2,1,0:T(8,128)}, f32[2,1,768,192]{2,3,1,0:T(8,128)}) async-done(((f32[2,1,192,576]{3,2,1,0:T(8,128)}, f32[2,1,192,768]{3,2,1,0:T(8,128)}, f32[2,1,768,192]{2,3,1,0:T(8,128)}), (f32[2,1,192,576]{3,2,1,0:T(8,128)}, f32[2,1,192,768]{3,2,1,0:T(8,128)}, f32[2,1,768,192]{2,3,1,0:T(8,128)})) %all-reduce.12.cloned.1.call-update) | async-done | bytes 3244048 | tf_op jit(solution)/shard_map/psum | solution.py:371
  (466 shorter events, 406.7 us)
Async XLA Ops:
  7.2 16.0 %all-to-all-start = ((bf16[4,512,192]{1,2,0:T(8,128)(2,1)}), bf16[4,512,192]{1,2,0:T(8,128)(2,1)S(1)}, u32[]{:S(2)}, u32[]{:S(2)}) async-start(bf16[4,512,192]{1,2,0:T(8,128)(2,1)} %param.15), calls=%async_computation | async-start | bytes 1572864 | tf_op jit(solution)/shard_map/all_to_all | solution.py:137
  23.2 15.1 %all-to-all-start.3 = ((bf16[4,512,192]{1,2,0:T(8,128)(2,1)}), bf16[4,512,192]{1,2,0:T(8,128)(2,1)S(1)}, u32[]{:S(2)}, u32[]{:S(2)}) async-start(bf16[4,512,192]{1,2,0:T(8,128)(2,1)} %bitcast.407), calls=%async_computation.3 | async-start | bytes 1572864 | tf_op jit(solution)/shard_map/all_to_all | solution.py:135
  38.3 15.9 %all-to-all-start.2 = ((bf16[4,512,192]{1,2,0:T(8,128)(2,1)}), bf16[4,512,192]{1,2,0:T(8,128)(2,1)}, u32[]{:S(2)}, u32[]{:S(2)}) async-start(bf16[4,512,192]{1,2,0:T(8,128)(2,1)} %bitcast.408), calls=%async_computation.2 | async-start | bytes 1572864 | tf_op jit(solution)/shard_map/all_to_all | solution.py:134
  54.2 15.1 %all-to-all-start.1 = ((bf16[4,512,192]{1,2,0:T(8,128)(2,1)}), bf16[4,512,192]{1,2,0:T(8,128)(2,1)S(1)}, u32[]{:S(2)}, u32[]{:S(2)}) async-start(bf16[4,512,192]{1,2,0:T(8,128)(2,1)} %bitcast.409), calls=%async_computation.1 | async-start | bytes 1572864 | tf_op jit(solution)/shard_map/all_to_all | solution.py:136
  86.8 15.1 %all-to-all-start.4 = ((bf16[4,2,49152]{2,1,0:T(2,128)(2,1)}), bf16[4,2,49152]{2,1,0:T(2,128)(2,1)S(1)}, u32[]{:S(2)}, u32[]{:S(2)}) async-start(bf16[4,2,49152]{2,1,0:T(2,128)(2,1)} %reshape.507), calls=%async_computation.4 | async-start | bytes 1572864 | tf_op jit(solution)/shard_map/all_to_all | solution.py:157
  91.0 40.6 %copy-start.82 = (f32[1,192]{1,0:T(1,128)}, f32[1,192]{1,0:T(1,128)S(1)}, u32[]{:S(2)}) copy-start(f32[1,192]{1,0:T(1,128)S(1)} %get-tuple-element.289) | copy-start | bytes 2308
  133.5 15.1 %all-to-all-start.5 = ((bf16[4,512,192]{1,2,0:T(8,128)(2,1)}), bf16[4,512,192]{1,2,0:T(8,128)(2,1)S(1)}, u32[]{:S(2)}, u32[]{:S(2)}) async-start(bf16[4,512,192]{1,2,0:T(8,128)(2,1)} %bitcast.406), calls=%async_computation.5 | async-start | bytes 1572864 | tf_op jit(solution)/shard_map/all_to_all | solution.py:137
  148.7 15.3 %all-to-all-start.8 = ((bf16[4,512,192]{1,2,0:T(8,128)(2,1)}), bf16[4,512,192]{1,2,0:T(8,128)(2,1)S(1)}, u32[]{:S(2)}, u32[]{:S(2)}) async-start(bf16[4,512,192]{1,2,0:T(8,128)(2,1)} %bitcast.403), calls=%async_computation.8 | async-start | bytes 1572864 | tf_op jit(solution)/shard_map/all_to_all | solution.py:135
  164.0 15.9 %all-to-all-start.7 = ((bf16[4,512,192]{1,2,0:T(8,128)(2,1)}), bf16[4,512,192]{1,2,0:T(8,128)(2,1)}, u32[]{:S(2)}, u32[]{:S(2)}) async-start(bf16[4,512,192]{1,2,0:T(8,128)(2,1)} %bitcast.404), calls=%async_computation.7 | async-start | bytes 1572864 | tf_op jit(solution)/shard_map/all_to_all | solution.py:134
  179.9 15.1 %all-to-all-start.6 = ((bf16[4,512,192]{1,2,0:T(8,128)(2,1)}), bf16[4,512,192]{1,2,0:T(8,128)(2,1)S(1)}, u32[]{:S(2)}, u32[]{:S(2)}) async-start(bf16[4,512,192]{1,2,0:T(8,128)(2,1)} %bitcast.405), calls=%async_computation.6 | async-start | bytes 1572864 | tf_op jit(solution)/shard_map/all_to_all | solution.py:136
  216.3 15.9 %all-to-all-start.9 = ((bf16[4,2,49152]{2,1,0:T(2,128)(2,1)}), bf16[4,2,49152]{2,1,0:T(2,128)(2,1)}, u32[]{:S(2)}, u32[]{:S(2)}) async-start(bf16[4,2,49152]{2,1,0:T(2,128)(2,1)} %reshape.509), calls=%async_computation.9 | async-start | bytes 1572864 | tf_op jit(solution)/shard_map/all_to_all | solution.py:157
  221.9 45.1 %copy-start.14 = (f32[4,24,8,512]{3,2,0,1:T(8,128)}, f32[4,24,8,512]{3,2,0,1:T(8,128)S(1)}, u32[]{:S(2)}) copy-start(f32[4,24,8,512]{3,2,0,1:T(8,128)S(1)} %copy.217) | copy-start | bytes 4718596
  292.8 15.9 %all-to-all-start.10 = ((bf16[4,512,192]{1,2,0:T(8,128)(2,1)}), bf16[4,512,192]{1,2,0:T(8,128)(2,1)}, u32[]{:S(2)}, u32[]{:S(2)}) async-start(bf16[4,512,192]{1,2,0:T(8,128)(2,1)} %bitcast.474), calls=%async_computation.10 | async-start | bytes 1572864 | tf_op jit(solution)/shard_map/all_to_all | solution.py:253
  339.1 26.0 %all-to-all-start.13 = ((bf16[4,2,49152]{2,1,0:T(2,128)(2,1)}), bf16[4,2,49152]{2,1,0:T(2,128)(2,1)S(1)}, u32[]{:S(2)}, u32[]{:S(2)}) async-start(bf16[4,2,49152]{2,1,0:T(2,128)(2,1)} %reshape.517), calls=%async_computation.13 | async-start | bytes 1572864 | tf_op jit(solution)/shard_map/all_to_all | solution.py:281
  365.1 28.2 %all-to-all-start.14 = ((bf16[4,2,49152]{2,1,0:T(2,128)(2,1)}), bf16[4,2,49152]{2,1,0:T(2,128)(2,1)}, u32[]{:S(2)}, u32[]{:S(2)}) async-start(bf16[4,2,49152]{2,1,0:T(2,128)(2,1)} %reshape.511), calls=%async_computation.14 | async-start | bytes 1572864 | tf_op jit(solution)/shard_map/all_to_all | solution.py:282
  393.3 18.5 %all-to-all-start.12 = ((bf16[4,2,49152]{2,1,0:T(2,128)(2,1)}), bf16[4,2,49152]{2,1,0:T(2,128)(2,1)}, u32[]{:S(2)}, u32[]{:S(2)}) async-start(bf16[4,2,49152]{2,1,0:T(2,128)(2,1)} %reshape.515), calls=%async_computation.12 | async-start | bytes 1572864 | tf_op jit(solution)/shard_map/all_to_all | solution.py:280
  411.8 22.0 %all-to-all-start.11 = ((bf16[4,2,49152]{2,1,0:T(2,128)(2,1)}), bf16[4,2,49152]{2,1,0:T(2,128)(2,1)}, u32[]{:S(2)}, u32[]{:S(2)}) async-start(bf16[4,2,49152]{2,1,0:T(2,128)(2,1)} %reshape.513), calls=%async_computation.11 | async-start | bytes 1572864 | tf_op jit(solution)/shard_map/all_to_all | solution.py:279
  463.8 16.3 %all-to-all-start.15 = ((bf16[4,512,192]{1,2,0:T(8,128)(2,1)}), bf16[4,512,192]{1,2,0:T(8,128)(2,1)}, u32[]{:S(2)}, u32[]{:S(2)}) async-start(bf16[4,512,192]{1,2,0:T(8,128)(2,1)} %bitcast.473), calls=%async_computation.15 | async-start | bytes 1572864 | tf_op jit(solution)/shard_map/all_to_all | solution.py:253
  512.8 29.3 %all-to-all-start.18 = ((bf16[4,2,49152]{2,1,0:T(2,128)(2,1)}), bf16[4,2,49152]{2,1,0:T(2,128)(2,1)}, u32[]{:S(2)}, u32[]{:S(2)}) async-start(bf16[4,2,49152]{2,1,0:T(2,128)(2,1)} %reshape.525), calls=%async_computation.18 | async-start | bytes 1572864 | tf_op jit(solution)/shard_map/all_to_all | solution.py:281
  542.1 25.9 %all-to-all-start.17 = ((bf16[4,2,49152]{2,1,0:T(2,128)(2,1)}), bf16[4,2,49152]{2,1,0:T(2,128)(2,1)}, u32[]{:S(2)}, u32[]{:S(2)}) async-start(bf16[4,2,49152]{2,1,0:T(2,128)(2,1)} %reshape.523), calls=%async_computation.17 | async-start | bytes 1572864 | tf_op jit(solution)/shard_map/all_to_all | solution.py:280
  546.3 160.1 %all-reduce.10.cloned.1.call-start = ((), (), s32[]{:S(2)}) async-start(), calls=%async_computation.20 | async-start | bytes 9437184 | tf_op jit(solution)/shard_map/psum | solution.py:384
  568.0 19.9 %all-to-all-start.16 = ((bf16[4,2,49152]{2,1,0:T(2,128)(2,1)}), bf16[4,2,49152]{2,1,0:T(2,128)(2,1)}, u32[]{:S(2)}, u32[]{:S(2)}) async-start(bf16[4,2,49152]{2,1,0:T(2,128)(2,1)} %reshape.521), calls=%async_computation.16 | async-start | bytes 1572864 | tf_op jit(solution)/shard_map/all_to_all | solution.py:279
  572.2 268.6 %all-reduce.12.cloned.1.call-start = ((), (), s32[]{:S(2)}) async-start(), calls=%async_computation.21 | async-start | bytes 6684672 | tf_op jit(solution)/shard_map/psum | solution.py:371
  610.0 51.5 %all-to-all-start.19 = ((bf16[4,2,49152]{2,1,0:T(2,128)(2,1)}), bf16[4,2,49152]{2,1,0:T(2,128)(2,1)}, u32[]{:S(2)}, u32[]{:S(2)}) async-start(bf16[4,2,49152]{2,1,0:T(2,128)(2,1)} %reshape.519), calls=%async_computation.19 | async-start | bytes 1572864 | tf_op jit(solution)/shard_map/all_to_all | solution.py:282
  (109 other events, 709.6 us)
Sparse Core Ops, SparseCore 0:
  553.3 147.5 all-reduce.9
  706.6 134.1 all-reduce.11
where the time goes:
time: 869 us; the launch traced here: 858 us
  waiting for transfers between devices  219 us (25%)
  matrix products  162 us (19%)
  local copies, waits for them, and re-layouts  131 us (15%)
  blocking collectives  127 us (15%)
  other arithmetic  121 us (14%)
  starting transfers between devices  81.2 us (9%)
  between operations  16.6 us (2%)
    psum x1, waiting for transfers between devices, shards(): lax.psum((stacked[0], stacked[1], stacked[6], stacked[7], stacked[8], sta...  134 us
    unnamed x270, local copies, waits for them, and re-layouts  76.3 us
    unnamed x11, other arithmetic  62.1 us
    psum x1, blocking collectives, shards(): lax.psum((stacked[2], stacked[3], stacked[4], stacked[5]), ('dp', 'grp'))  47.1 us
    psum x1, blocking collectives, shards(): lax.psum((stacked[0], stacked[1], stacked[6], stacked[7], stacked[8], sta...  37.8 us
    dot_general x2, matrix products, layer_forward(): jnp.dot(group_rows, widen_weight[layer_params, 0], preferred_element_type...  31.7 us
    psum x2, blocking collectives, layer_backward(): total_sum, total_cross = lax.psum((part_sum, part_cross), 'grp')  22.2 us
    sub x2, matrix products, single(): expon = jnp.exp(scores - highest)  21.1 us
  transfers between devices with their start and end apart: 22, of which 13 were waited for; matrix products, arithmetic and copies ran while one was open for 25% of the time, Pallas kernels for 0%

commit v1 on v0

--- a/solution.py
+++ b/solution.py
@@ -381,7 +381,9 @@
         ),
         "dp",
     )
-    shared_totals = lax.psum((stacked[2], stacked[3], stacked[4], stacked[5]), ("dp", "grp"))
+    shared_totals = lax.psum(
+        lax.psum((stacked[2], stacked[3], stacked[4], stacked[5]), "grp"), "dp"
+    )
     return (
         final.astype(jnp.bfloat16),
         outgrad,

time: 869 us -> 953 us (1.097)
  waiting for transfers between devices: 219 us -> 329 us
  blocking collectives: 127 us -> 101 us
    psum x1, waiting for transfers between devices: 0.01 us -> 55.5 us  [shards(): lax.psum((stacked[2], stacked[3], stacked[4], stacked[5]), 'grp')]
    psum x1, waiting for transfers between devices: 134 us -> 184 us  [shards(): lax.psum((stacked[0], stacked[1], stacked[6], stacked[7], stacked[8], sta...]
    psum x1, blocking collectives: 47.1 us -> 17.8 us  [shards(): lax.psum((stacked[2], stacked[3], stacked[4], stacked[5]), 'grp')]
  transfers between devices with their start and end apart: 22 -> 22, of which waited for: 13 -> 15; matrix products, arithmetic and copies ran while one was open for 25% -> 23% of each run, Pallas kernels for 0% -> 0%
where the time goes in v1:
time: 953 us; the launch traced here: 943 us
  waiting for transfers between devices  329 us (35%)
  matrix products  162 us (17%)
  local copies, waits for them, and re-layouts  132 us (14%)
  other arithmetic  121 us (13%)
  blocking collectives  101 us (11%)
  starting transfers between devices  81.2 us (9%)
  between operations  16.6 us (2%)
    psum x1, waiting for transfers between devices, shards(): lax.psum((stacked[0], stacked[1], stacked[6], stacked[7], stacked[8], sta...  184 us
    unnamed x270, local copies, waits for them, and re-layouts  77.1 us
    unnamed x11, other arithmetic  62.7 us
    psum x1, waiting for transfers between devices, shards(): lax.psum((stacked[2], stacked[3], stacked[4], stacked[5]), 'grp')  55.5 us
    psum x1, blocking collectives, shards(): lax.psum((stacked[0], stacked[1], stacked[6], stacked[7], stacked[8], sta...  40.7 us
    dot_general x2, matrix products, layer_forward(): jnp.dot(group_rows, widen_weight[layer_params, 0], preferred_element_type...  31.7 us
    psum x2, blocking collectives, layer_backward(): total_sum, total_cross = lax.psum((part_sum, part_cross), 'grp')  22.2 us
    sub x2, matrix products, single(): expon = jnp.exp(scores - highest)  21.1 us
  transfers between devices with their start and end apart: 22, of which 15 were waited for; matrix products, arithmetic and copies ran while one was open for 23% of the time, Pallas kernels for 0%

profile of v1, /device:TPU:0, one launch (start us, length us, event | category | flops | bytes accessed | tf_op | source)
XLA Modules:
  0.0 942.7 jit_solution(5546048368971954384)
XLA Ops:
  31.4 6.9 all-to-all-done.3
  45.1 9.1 all-to-all-done.2
  57.7 10.6 %fusion.129 = (f32[12,512]{1,0:T(8,128)S(1)}, f32[12,512,512]{1,2,0:T(8,128)}) fusion(pred[512]{0:T(512)(128)(4,1)S(1)} %iota_compare_fusion, bf16[512,12,64]{0,2,1:T(8,128)(2,1)} %bitcast.12, bf16[512,12,64]{0,2,1:T(8,128)(2,1)S(1)} %bitcast.431), kind=kOutput, calls=%fused_computation.281 | convolution fusion | flops 415236608 | bytes 14180864 | tf_op jit(solution)/shard_map/while/body/eval_jaxpr/sub | solution.py:42
  91.6 10.4 %all-to-all-done.4 = bf16[4,2,49152]{2,1,0:T(2,128)(2,1)S(1)} async-done(((bf16[4,2,49152]{2,1,0:T(2,128)(2,1)}), bf16[4,2,49152]{2,1,0:T(2,128)(2,1)S(1)}, u32[]{:S(2)}, u32[]{:S(2)}) %all-to-all-start.4) | async-done | bytes 786464 | tf_op jit(solution)/shard_map/all_to_all | solution.py:157
  103.8 15.9 %fusion.6 = (bf16[2048,768]{1,0:T(8,128)(2,1)S(1)}, f32[2048,768]{1,0:T(8,128)}) fusion(f32[768]{0:T(1024)S(1)} %get-tuple-element.241, bf16[2048,192]{0,1:T(8,128)(2,1)S(1)} %bitcast.493, bf16[2,1,192,768]{3,2,1,0:T(8,128)(2,1)S(1)} %copy-done.66), kind=kOutput, calls=%fused_computation.18 | convolution fusion | flops 707788800 | bytes 10522624 | tf_op jit(solution)/shard_map/dot_general | solution.py:160
  121.4 10.1 %all-reduce.6 = (f32[2048]{0:T(1024)S(1)}, f32[2048]{0:T(1024)S(1)}) all-reduce(f32[2048]{0:T(1024)S(1)} %get-tuple-element.233, f32[2048]{0:T(1024)S(1)} %get-tuple-element.232), channel_id=1, replica_groups=mesh['dp'=8,'grp'=4] {'grp'}, use_global_device_ids=true, to_apply=%region_7.8 | all-reduce | flops 4096 | bytes 32768 | tf_op jit(solution)/shard_map/psum | solution.py:171
  155.5 8.5 all-to-all-done.8
  171.0 8.9 all-to-all-done.7
  183.4 10.5 %fusion.131 = (f32[12,512]{1,0:T(8,128)S(1)}, f32[12,512,512]{1,2,0:T(8,128)}) fusion(pred[512]{0:T(512)(128)(4,1)S(1)} %iota_compare_fusion, bf16[512,12,64]{0,2,1:T(8,128)(2,1)} %bitcast.37, bf16[512,12,64]{0,2,1:T(8,128)(2,1)S(1)} %bitcast.433), kind=kOutput, calls=%fused_computation.283 | convolution fusion | flops 415236608 | bytes 14180864 | tf_op jit(solution)/shard_map/while/body/eval_jaxpr/sub | solution.py:42
  221.9 10.4 %all-to-all-done.9 = bf16[4,2,49152]{2,1,0:T(2,128)(2,1)} async-done(((bf16[4,2,49152]{2,1,0:T(2,128)(2,1)}), bf16[4,2,49152]{2,1,0:T(2,128)(2,1)}, u32[]{:S(2)}, u32[]{:S(2)}) %all-to-all-start.9) | async-done | bytes 786464 | tf_op jit(solution)/shard_map/all_to_all | solution.py:157
  238.5 15.8 %fusion.9 = (bf16[2048,768]{1,0:T(8,128)(2,1)S(1)}, f32[2048,768]{1,0:T(8,128)}) fusion(f32[768]{0:T(1024)S(1)} %get-tuple-element.240, bf16[2048,192]{0,1:T(8,128)(2,1)S(1)} %bitcast.497, bf16[2,1,192,768]{3,2,1,0:T(8,128)(2,1)S(1)} %copy-done.67), kind=kOutput, calls=%fused_computation.21 | convolution fusion | flops 707788800 | bytes 10522624 | tf_op jit(solution)/shard_map/dot_general | solution.py:160
  256.7 10.3 %all-reduce.5 = (f32[2048]{0:T(1024)S(1)}, f32[2048]{0:T(1024)S(1)}) all-reduce(f32[2048]{0:T(1024)S(1)} %get-tuple-element.231, f32[2048]{0:T(1024)S(1)} %get-tuple-element.230), channel_id=1, replica_groups=mesh['dp'=8,'grp'=4] {'grp'}, use_global_device_ids=true, to_apply=%region_15.16 | all-reduce | flops 4096 | bytes 32768 | tf_op jit(solution)/shard_map/psum | solution.py:171
  269.4 10.3 %all-reduce.4 = (f32[2048]{0:T(1024)S(1)}, f32[2048]{0:T(1024)S(1)}) all-reduce(f32[2048]{0:T(1024)S(1)} %get-tuple-element.223, f32[2048]{0:T(1024)S(1)} %bitcast.523), channel_id=1, replica_groups=mesh['dp'=8,'grp'=4] {'grp'}, use_global_device_ids=true, to_apply=%region_19.20 | all-reduce | flops 4096 | bytes 32768 | tf_op jit(solution)/shard_map/psum | solution.py:237
  297.1 11.6 %all-to-all-done.10 = bf16[4,512,192]{1,2,0:T(8,128)(2,1)} async-done(((bf16[4,512,192]{1,2,0:T(8,128)(2,1)}), bf16[4,512,192]{1,2,0:T(8,128)(2,1)}, u32[]{:S(2)}, u32[]{:S(2)}) %all-to-all-start.10) | async-done | bytes 786464 | tf_op jit(solution)/shard_map/all_to_all | solution.py:253
  342.8 11.6 %multiply_reduce_fusion.1 = (f32[12,512]{1,0:T(8,128)S(1)}, f32[12,512,512]{1,2,0:T(8,128)}) fusion(f32[12,512,512]{1,2,0:T(8,128)} %get-tuple-element.306, f32[12,512]{1,0:T(8,128)S(1)} %get-tuple-element.305, bf16[512,12,64]{0,2,1:T(8,128)(2,1)} %bitcast.513, bf16[512,12,64]{0,2,1:T(8,128)(2,1)} %bitcast.510), kind=kOutput, calls=%fused_computation.5 | convolution fusion | flops 412084224 | bytes 26787840 | tf_op jit(solution)/shard_map/while/body/eval_jaxpr/qhd,khd->hqk/dot_general | solution.py:61
  369.6 9.6 %multiply_convert_fusion.1 = bf16[12,512,512]{1,2,0:T(8,128)(2,1)S(1)} fusion(f32[12,512,512]{1,2,0:T(8,128)} %get-tuple-element.313, f32[12,512]{1,0:T(8,128)S(1)} %get-tuple-element.312, f32[12,512,512]{1,2,0:T(8,128)} %get-tuple-element.306, f32[12,512]{1,0:T(8,128)S(1)} %get-tuple-element.305), kind=kLoop, calls=%fused_computation.4 | loop fusion | flops 12582912 | bytes 31506432 | tf_op jit(solution)/shard_map/while/body/eval_jaxpr/convert_element_type | solution.py:65
  440.9 11.9 %all-reduce.3 = (f32[2048]{0:T(1024)S(1)}, f32[2048]{0:T(1024)S(1)}) all-reduce(f32[2048]{0:T(1024)S(1)} %get-tuple-element.221, f32[2048]{0:T(1024)S(1)} %get-tuple-element.228), channel_id=1, replica_groups=mesh['dp'=8,'grp'=4] {'grp'}, use_global_device_ids=true, to_apply=%region_26.27 | all-reduce | flops 4096 | bytes 32768 | tf_op jit(solution)/shard_map/psum | solution.py:237
  495.8 8.9 multiply_reduce_fusion
  517.1 9.6 %multiply_convert_fusion = bf16[12,512,512]{1,2,0:T(8,128)(2,1)S(1)} fusion(f32[12,512,512]{1,2,0:T(8,128)} %get-tuple-element.316, f32[12,512]{1,0:T(8,128)S(1)} %get-tuple-element.315, f32[12,512,512]{1,2,0:T(8,128)} %get-tuple-element.299, f32[12,512]{1,0:T(8,128)S(1)} %copy-done.81), kind=kLoop, calls=%fused_computation.2 | loop fusion | flops 12582912 | bytes 31506432 | tf_op jit(solution)/shard_map/while/body/eval_jaxpr/convert_element_type | solution.py:65
  558.1 8.0 reduce.35
  600.3 55.5 %all-reduce.10.cloned.1.call-done = f32[2,768,768]{2,1,0:T(8,128)} async-done(((f32[2,768,768]{2,1,0:T(8,128)}), f32[2,768,768]{2,1,0:T(8,128)}) %all-reduce.10.cloned.1.call-update) | async-done | bytes 4718608 | tf_op jit(solution)/shard_map/psum | solution.py:385
  675.7 17.8 %all-reduce.2 = (f32[2,768]{1,0:T(2,128)S(1)}, f32[2,768]{1,0:T(2,128)S(1)}, f32[2,768]{1,0:T(2,128)S(1)}) all-reduce(f32[2,768]{1,0:T(2,128)S(1)} %pad_maximum_fusion.4, f32[2,768]{1,0:T(2,128)S(1)} %pad_maximum_fusion.5, f32[2,768]{1,0:T(2,128)S(1)} %pad_maximum_fusion.6), channel_id=1, replica_groups=mesh['dp'=8,'grp'=4] {'grp'}, use_global_device_ids=true, to_apply=%region_40.41 | all-reduce | flops 4608 | bytes 36864 | tf_op jit(solution)/shard_map/psum | solution.py:385
  700.7 40.7 %all-reduce = (f32[2,2,192]{2,1,0:T(2,128)}, f32[2,768]{1,0:T(2,128)}, f32[2,768]{1,0:T(2,128)}, f32[2,768]{1,0:T(2,128)}, f32[2,768]{1,0:T(2,128)}, /*index=5*/...) all-reduce(f32[2,2,192]{2,1,0:T(2,128)S(1)} %pad_maximum_fusion.8, ...), channel_id=1, replica_groups=mesh['dp'=8,'grp'=4] {'dp'}, use_global_device_ids=true, to_apply=%region_35.36 | all-reduce | flops 8064 | bytes 64512 | tf_op jit(solution)/shard_map/psum | solution.py:371
  741.4 184.1 %all-reduce.12.cloned.1.call-done = (f32[2,1,192,576]{3,2,1,0:T(8,128)}, f32[2,768,768]{2,1,0:T(8,128)}, f32[2,1,192,768]{3,2,1,0:T(8,128)}, f32[2,1,768,192]{2,3,1,0:T(8,128)}) async-done(((f32[2,1,192,576]{3,2,1,0:T(8,128)}, f32[2,768,768]{2,1,0:T(8,128)}, f32[2,1,192,768]{3,2,1,0:T(8,128)}, f32[2,1,768,192]{2,3,1,0:T(8,128)}), (f32[2,1,192,576]{3,2,1,0:T(8,128)}, f32[2,768,768]{2,1,0:T(8,128)}, ...) | async-done | bytes 7962640 | tf_op jit(solution)/shard_map/psum | solution.py:371
  (466 shorter events, 418.9 us)
Async XLA Ops:
  7.2 16.0 %all-to-all-start = ((bf16[4,512,192]{1,2,0:T(8,128)(2,1)}), bf16[4,512,192]{1,2,0:T(8,128)(2,1)S(1)}, u32[]{:S(2)}, u32[]{:S(2)}) async-start(bf16[4,512,192]{1,2,0:T(8,128)(2,1)} %param.15), calls=%async_computation | async-start | bytes 1572864 | tf_op jit(solution)/shard_map/all_to_all | solution.py:137
  23.2 15.1 %all-to-all-start.3 = ((bf16[4,512,192]{1,2,0:T(8,128)(2,1)}), bf16[4,512,192]{1,2,0:T(8,128)(2,1)S(1)}, u32[]{:S(2)}, u32[]{:S(2)}) async-start(bf16[4,512,192]{1,2,0:T(8,128)(2,1)} %bitcast.407), calls=%async_computation.3 | async-start | bytes 1572864 | tf_op jit(solution)/shard_map/all_to_all | solution.py:135
  38.3 15.9 %all-to-all-start.2 = ((bf16[4,512,192]{1,2,0:T(8,128)(2,1)}), bf16[4,512,192]{1,2,0:T(8,128)(2,1)}, u32[]{:S(2)}, u32[]{:S(2)}) async-start(bf16[4,512,192]{1,2,0:T(8,128)(2,1)} %bitcast.408), calls=%async_computation.2 | async-start | bytes 1572864 | tf_op jit(solution)/shard_map/all_to_all | solution.py:134
  54.2 15.1 %all-to-all-start.1 = ((bf16[4,512,192]{1,2,0:T(8,128)(2,1)}), bf16[4,512,192]{1,2,0:T(8,128)(2,1)S(1)}, u32[]{:S(2)}, u32[]{:S(2)}) async-start(bf16[4,512,192]{1,2,0:T(8,128)(2,1)} %bitcast.409), calls=%async_computation.1 | async-start | bytes 1572864 | tf_op jit(solution)/shard_map/all_to_all | solution.py:136
  86.9 15.1 %all-to-all-start.4 = ((bf16[4,2,49152]{2,1,0:T(2,128)(2,1)}), bf16[4,2,49152]{2,1,0:T(2,128)(2,1)S(1)}, u32[]{:S(2)}, u32[]{:S(2)}) async-start(bf16[4,2,49152]{2,1,0:T(2,128)(2,1)} %reshape.507), calls=%async_computation.4 | async-start | bytes 1572864 | tf_op jit(solution)/shard_map/all_to_all | solution.py:157
  91.0 40.6 %copy-start.82 = (f32[1,192]{1,0:T(1,128)}, f32[1,192]{1,0:T(1,128)S(1)}, u32[]{:S(2)}) copy-start(f32[1,192]{1,0:T(1,128)S(1)} %get-tuple-element.293) | copy-start | bytes 2308
  133.5 15.1 %all-to-all-start.5 = ((bf16[4,512,192]{1,2,0:T(8,128)(2,1)}), bf16[4,512,192]{1,2,0:T(8,128)(2,1)S(1)}, u32[]{:S(2)}, u32[]{:S(2)}) async-start(bf16[4,512,192]{1,2,0:T(8,128)(2,1)} %bitcast.406), calls=%async_computation.5 | async-start | bytes 1572864 | tf_op jit(solution)/shard_map/all_to_all | solution.py:137
  148.7 15.3 %all-to-all-start.8 = ((bf16[4,512,192]{1,2,0:T(8,128)(2,1)}), bf16[4,512,192]{1,2,0:T(8,128)(2,1)S(1)}, u32[]{:S(2)}, u32[]{:S(2)}) async-start(bf16[4,512,192]{1,2,0:T(8,128)(2,1)} %bitcast.403), calls=%async_computation.8 | async-start | bytes 1572864 | tf_op jit(solution)/shard_map/all_to_all | solution.py:135
  164.0 15.9 %all-to-all-start.7 = ((bf16[4,512,192]{1,2,0:T(8,128)(2,1)}), bf16[4,512,192]{1,2,0:T(8,128)(2,1)}, u32[]{:S(2)}, u32[]{:S(2)}) async-start(bf16[4,512,192]{1,2,0:T(8,128)(2,1)} %bitcast.404), calls=%async_computation.7 | async-start | bytes 1572864 | tf_op jit(solution)/shard_map/all_to_all | solution.py:134
  179.9 15.1 %all-to-all-start.6 = ((bf16[4,512,192]{1,2,0:T(8,128)(2,1)}), bf16[4,512,192]{1,2,0:T(8,128)(2,1)S(1)}, u32[]{:S(2)}, u32[]{:S(2)}) async-start(bf16[4,512,192]{1,2,0:T(8,128)(2,1)} %bitcast.405), calls=%async_computation.6 | async-start | bytes 1572864 | tf_op jit(solution)/shard_map/all_to_all | solution.py:136
  216.3 15.9 %all-to-all-start.9 = ((bf16[4,2,49152]{2,1,0:T(2,128)(2,1)}), bf16[4,2,49152]{2,1,0:T(2,128)(2,1)}, u32[]{:S(2)}, u32[]{:S(2)}) async-start(bf16[4,2,49152]{2,1,0:T(2,128)(2,1)} %reshape.509), calls=%async_computation.9 | async-start | bytes 1572864 | tf_op jit(solution)/shard_map/all_to_all | solution.py:157
  221.9 45.1 %copy-start.14 = (f32[4,24,8,512]{3,2,0,1:T(8,128)}, f32[4,24,8,512]{3,2,0,1:T(8,128)S(1)}, u32[]{:S(2)}) copy-start(f32[4,24,8,512]{3,2,0,1:T(8,128)S(1)} %copy.217) | copy-start | bytes 4718596
  292.8 15.9 %all-to-all-start.10 = ((bf16[4,512,192]{1,2,0:T(8,128)(2,1)}), bf16[4,512,192]{1,2,0:T(8,128)(2,1)}, u32[]{:S(2)}, u32[]{:S(2)}) async-start(bf16[4,512,192]{1,2,0:T(8,128)(2,1)} %bitcast.474), calls=%async_computation.10 | async-start | bytes 1572864 | tf_op jit(solution)/shard_map/all_to_all | solution.py:253
  339.1 26.0 %all-to-all-start.13 = ((bf16[4,2,49152]{2,1,0:T(2,128)(2,1)}), bf16[4,2,49152]{2,1,0:T(2,128)(2,1)S(1)}, u32[]{:S(2)}, u32[]{:S(2)}) async-start(bf16[4,2,49152]{2,1,0:T(2,128)(2,1)} %reshape.517), calls=%async_computation.13 | async-start | bytes 1572864 | tf_op jit(solution)/shard_map/all_to_all | solution.py:281
  365.0 28.2 %all-to-all-start.14 = ((bf16[4,2,49152]{2,1,0:T(2,128)(2,1)}), bf16[4,2,49152]{2,1,0:T(2,128)(2,1)}, u32[]{:S(2)}, u32[]{:S(2)}) async-start(bf16[4,2,49152]{2,1,0:T(2,128)(2,1)} %reshape.511), calls=%async_computation.14 | async-start | bytes 1572864 | tf_op jit(solution)/shard_map/all_to_all | solution.py:282
  393.2 18.5 %all-to-all-start.12 = ((bf16[4,2,49152]{2,1,0:T(2,128)(2,1)}), bf16[4,2,49152]{2,1,0:T(2,128)(2,1)}, u32[]{:S(2)}, u32[]{:S(2)}) async-start(bf16[4,2,49152]{2,1,0:T(2,128)(2,1)} %reshape.515), calls=%async_computation.12 | async-start | bytes 1572864 | tf_op jit(solution)/shard_map/all_to_all | solution.py:280
  411.7 22.0 %all-to-all-start.11 = ((bf16[4,2,49152]{2,1,0:T(2,128)(2,1)}), bf16[4,2,49152]{2,1,0:T(2,128)(2,1)}, u32[]{:S(2)}, u32[]{:S(2)}) async-start(bf16[4,2,49152]{2,1,0:T(2,128)(2,1)} %reshape.513), calls=%async_computation.11 | async-start | bytes 1572864 | tf_op jit(solution)/shard_map/all_to_all | solution.py:279
  463.8 16.3 %all-to-all-start.15 = ((bf16[4,512,192]{1,2,0:T(8,128)(2,1)}), bf16[4,512,192]{1,2,0:T(8,128)(2,1)}, u32[]{:S(2)}, u32[]{:S(2)}) async-start(bf16[4,512,192]{1,2,0:T(8,128)(2,1)} %bitcast.473), calls=%async_computation.15 | async-start | bytes 1572864 | tf_op jit(solution)/shard_map/all_to_all | solution.py:253
  512.8 29.3 %all-to-all-start.18 = ((bf16[4,2,49152]{2,1,0:T(2,128)(2,1)}), bf16[4,2,49152]{2,1,0:T(2,128)(2,1)}, u32[]{:S(2)}, u32[]{:S(2)}) async-start(bf16[4,2,49152]{2,1,0:T(2,128)(2,1)} %reshape.525), calls=%async_computation.18 | async-start | bytes 1572864 | tf_op jit(solution)/shard_map/all_to_all | solution.py:281
  542.0 26.4 %all-to-all-start.17 = ((bf16[4,2,49152]{2,1,0:T(2,128)(2,1)}), bf16[4,2,49152]{2,1,0:T(2,128)(2,1)}, u32[]{:S(2)}, u32[]{:S(2)}) async-start(bf16[4,2,49152]{2,1,0:T(2,128)(2,1)} %reshape.523), calls=%async_computation.17 | async-start | bytes 1572864 | tf_op jit(solution)/shard_map/all_to_all | solution.py:280
  546.2 109.5 %all-reduce.10.cloned.1.call-start = ((), (), s32[]{:S(2)}) async-start(), calls=%async_computation.20 | async-start | bytes 9437184 | tf_op jit(solution)/shard_map/psum | solution.py:385
  568.5 24.8 %all-to-all-start.16 = ((bf16[4,2,49152]{2,1,0:T(2,128)(2,1)}), bf16[4,2,49152]{2,1,0:T(2,128)(2,1)}, u32[]{:S(2)}, u32[]{:S(2)}) async-start(bf16[4,2,49152]{2,1,0:T(2,128)(2,1)} %reshape.521), calls=%async_computation.16 | async-start | bytes 1572864 | tf_op jit(solution)/shard_map/all_to_all | solution.py:279
  572.7 352.9 %all-reduce.12.cloned.1.call-start = ((), (), s32[]{:S(2)}) async-start(), calls=%async_computation.21 | async-start | bytes 16121856 | tf_op jit(solution)/shard_map/psum | solution.py:371
  671.2 22.3 %all-to-all-start.19 = ((bf16[4,2,49152]{2,1,0:T(2,128)(2,1)}), bf16[4,2,49152]{2,1,0:T(2,128)(2,1)}, u32[]{:S(2)}, u32[]{:S(2)}) async-start(bf16[4,2,49152]{2,1,0:T(2,128)(2,1)} %reshape.519), calls=%async_computation.19 | async-start | bytes 1572864 | tf_op jit(solution)/shard_map/all_to_all | solution.py:282
  (109 other events, 708.3 us)
Sparse Core Ops, SparseCore 0:
  550.8 104.8 all-reduce.9
  661.3 264.1 all-reduce.11
